TPU v7x, 512 devices: a whole 4x8x8 slice. The times are simulated.
512 devices in a mesh: rows: 128 (over y_lo, x, z, core), rep: 4 (over y_hi).
Axes of the slice: x: 4, y: 8 (y_hi: 4, y_lo: 2; y = y_hi * 2 + y_lo), z: 8, core: 2. Of those that a mesh axis runs over, the one named last changes fastest.
Arguments:
- node_feats: bfloat16 [131072, 256], P('rows'), may hold values from -6 to 6
- weight: bfloat16 [256, 256], replicated, may hold values from -0.375 to 0.375
- cotangent: bfloat16 [131072, 256], P('rows'), may hold values from -6 to 6
- tile_values: bfloat16 [128, 5, 32, 128, 128], P('rows', None, 'rep'), may hold values from -1 to 1, as said below
- tile_coords: int32 [2, 128, 5, 32], P(None, 'rows', None, 'rep'), may hold values from 0 to 7, as said below
- tile_counts: int32 [128, 5], P('rows'), may hold values from 0 to 32, as said below
Outputs:
- activated: bfloat16 [131072, 256], P('rows')
- input_grad: bfloat16 [131072, 256], P('rows')
- weight_grad: float32 [256, 256], replicated
Inputs may be any that keep to these rules, and one draw needn't show every extreme that they name: tile_counts[r, d] = tile_counts[(r + d - 2) mod 128, 4 - d]; tile_counts[r, 2] = 32. tile_coords[0, r, d, k] = tile_coords[1, s, 4 - d, k] and tile_coords[1, r, d, k] = tile_coords[0, s, 4 - d, k] with s = (r + d - 2) mod 128, for d other than 2; for d = 2, slots 2m and 2m + 1 hold swapped coordinates. tile_values[r, d, k] is the transpose of tile_values[s, 4 - d, k] with s as above for d other than 2; for d = 2, slot 2m + 1 is the transpose of slot 2m.
All inputs are finite; a program needn't handle non-finite values.
Results may differ from a plain program's by a relative error of at most 0.006.
Values may be sent and summed in bfloat16 or wider, within the bound.
A program may use at most 64 MiB of HBM per device.

v0:
```python
import jax
import jax.numpy as jnp
from jax import lax
from jax.sharding import PartitionSpec as P


def shifted(x, axis, by):
    size = lax.axis_size(axis)
    return lax.ppermute(x, axis, [(i, (i + by) % size) for i in range(size)])


def silu_slope(value):
    sig = jax.nn.sigmoid(value)
    return sig * (1.0 + value * (1.0 - sig))


def offset_terms(panel, values, rows_idx, cols_idx, live):
    blocks = panel.shape[0]
    picked = panel[cols_idx]
    product = jnp.einsum("kuv,kvf->kuf", values, picked, preferred_element_type=jnp.float32)
    place = (
        (rows_idx[:, None] == jnp.arange(blocks, dtype=jnp.int32)[None, :]) & live[:, None]
    ).astype(jnp.float32)
    return jnp.einsum("kb,kuf->buf", place, product, precision=lax.Precision.HIGHEST)


def fetch_panel(source, offset):
    return shifted(source, "rows", -offset)


def propagate(source, values, rows_idx, cols_idx, counts):
    reach = values.shape[0]
    slots_dev = values.shape[1]
    tile = values.shape[-1]
    hops = reach // 2
    local_rows = source.shape[0]
    width = source.shape[1]
    blocks = local_rows // tile
    first_slot = lax.axis_index("rep") * slots_dev
    live = (first_slot + jnp.arange(slots_dev, dtype=jnp.int32))[None, :] < counts[:, None]
    total = jnp.zeros((blocks, tile, width), jnp.float32)
    for step in range(reach):
        offset = step - hops
        panel = source if offset == 0 else fetch_panel(source, offset)
        total = total + offset_terms(
            panel.reshape(blocks, tile, width),
            values[step],
            rows_idx[step],
            cols_idx[step],
            live[step],
        )
    return total.reshape(local_rows, width)


def per_device(node_feats, weight, cotangent, tile_values, tile_coords, tile_counts):
    values = tile_values[0]
    rows_idx = tile_coords[0, 0]
    cols_idx = tile_coords[1, 0]
    counts = tile_counts[0]
    scale = (node_feats.shape[0] * lax.axis_size("rows")) ** (-0.5)
    contract = (((0,), (0,)), ((), ()))
    transformed = jnp.dot(node_feats, weight, preferred_element_type=jnp.float32).astype(
        jnp.bfloat16
    )
    agg_part = propagate(transformed, values, rows_idx, cols_idx, counts)
    aggregated = lax.psum(agg_part, "rep")
    activated = jax.nn.silu(aggregated).astype(jnp.bfloat16)
    adjoint = (cotangent.astype(jnp.float32) * silu_slope(aggregated)).astype(jnp.bfloat16)
    back_part = propagate(adjoint, values, rows_idx, cols_idx, counts)
    back_sum = lax.psum(back_part, "rep").astype(jnp.bfloat16)
    grad_terms = (
        lax.dot_general(node_feats, back_sum, contract, preferred_element_type=jnp.float32) * scale
    )
    weight_grad = lax.psum(grad_terms, "rows")
    input_grad = jnp.dot(back_sum, weight.T, preferred_element_type=jnp.float32).astype(
        jnp.bfloat16
    )
    return (activated, input_grad, weight_grad)


def solution(mesh):
    return jax.shard_map(
        per_device,
        mesh=mesh,
        in_specs=(
            P("rows", None),
            P(),
            P("rows", None),
            P("rows", None, "rep", None, None),
            P(None, "rows", None, "rep"),
            P("rows", None),
        ),
        out_specs=(P("rows", None), P("rows", None), P()),
        check_vma=False,
    )
```

profile of v0, /device:TPU:1, one launch (start us, length us, event | category | flops | bytes accessed | tf_op | source)
XLA Modules:
  0.0 1200.1 jit_solution(11605175221021727507)
XLA Ops:
  7.2 1.0 copy-done
  8.2 2.0 convolution_convert_fusion.1
  10.2 4.8 collective-permute-start
  15.0 4.9 collective-permute-start.1
  19.9 2.9 collective-permute-start.2
  22.8 8.5 collective-permute-start.3
  31.3 0.7 fusion.89
  32.1 0.7 slice_bitcast_fusion.5
  32.9 1.6 gather_fusion.2
  35.0 1.4 copy.15
  36.8 1.6 gather_fusion
  38.8 1.4 copy.13
  40.2 1.6 gather_fusion.1
  42.2 1.4 copy.14
  43.6 1.6 gather_fusion.3
  45.6 1.4 copy.16
  46.9 1.6 gather_fusion.4
  48.9 1.4 copy.17
  50.3 1.9 fusion.11
  54.1 0.6 copy-done.7
  56.5 1.3 copy.10
  57.9 70.2 %all-reduce.4.cloned.1.call-done = f32[1024,256]{1,0:T(8,128)} async-done(((f32[1024,256]{1,0:T(8,128)}), f32[1024,256]{1,0:T(8,128)}) %all-reduce.4.cloned.1.call-update) | async-done | bytes 1048592 | tf_op jit(solution)/shard_map/psum | solution.py:66
  128.1 2.5 multiply_convert_fusion
  130.5 2.1 collective-permute-start.4
  132.6 5.1 collective-permute-start.5
  137.7 1.9 collective-permute-start.6
  139.6 6.4 collective-permute-start.7
  146.0 1.4 gather_fusion.7
  147.4 1.4 fusion.21
  148.8 1.4 copy.20
  150.2 2.4 gather_fusion.5
  152.6 1.4 fusion.29
  154.0 1.4 copy.18
  155.4 2.4 gather_fusion.6
  157.8 1.4 fusion.25
  159.2 1.4 copy.19
  160.6 2.4 gather_fusion.8
  163.0 1.4 fusion.17
  164.4 1.4 copy.21
  165.8 2.8 fusion.5
  168.6 1.6 gather_fusion.9
  170.6 1.4 copy.22
  172.0 1.9 convolution_add_fusion.3
  177.3 41.9 %all-reduce.7 = bf16[1024,256]{1,0:T(8,128)(2,1)S(1)} all-reduce(f32[1024,256]{1,0:T(8,128)S(1)} %bitcast.147), channel_id=1, replica_groups=mesh['rows'=128,'rep'=4] {'rep'}, use_global_device_ids=true, to_apply=%region_1.2 | all-reduce | flops 262144 | bytes 1572864 | tf_op jit(solution)/shard_map/psum | solution.py:70
  219.2 1.0 fusion
  220.3 1.1 convolution_convert_fusion
  221.4 970.1 %all-reduce.6.cloned.1.call-done = f32[256,256]{0,1:T(8,128)} async-done(((f32[256,256]{0,1:T(8,128)}), f32[256,256]{0,1:T(8,128)}) %all-reduce.6.cloned.1.call-update) | async-done | bytes 262160 | tf_op jit(solution)/shard_map/psum | solution.py:74
  1191.5 1.8 copy.12
  (58 shorter events, 9.8 us)
Async XLA Ops:
  7.2 1.0 copy-start
  7.2 27.3 %copy-start.1 = (bf16[1,5,8,128,128]{4,3,2,1,0:T(8,128)(2,1)S(1)}, bf16[1,5,8,128,128]{4,3,2,1,0:T(8,128)(2,1)}, u32[]{:S(2)}) copy-start(bf16[1,5,8,128,128]{4,3,2,1,0:T(8,128)(2,1)} %param.9) | copy-start | bytes 3932164
  7.2 120.9 %all-reduce.4.cloned.1.call-start = ((), (), s32[]{:S(2)}) async-start(), calls=%async_computation | async-start | bytes 2097152 | tf_op jit(solution)/shard_map/psum | solution.py:66
  10.2 26.6 %collective-permute-start = (bf16[1024,256]{1,0:T(8,128)(2,1)}, bf16[1024,256]{1,0:T(8,128)(2,1)}, u32[]{:S(2)}, u32[]{:S(2)}) collective-permute-start(bf16[1024,256]{1,0:T(8,128)(2,1)} %convolution_convert_fusion.1), channel_id=1, source_target_pairs={{0,8},{4,12},{8,16},{12,20},{16,24},{20,28},{24,32},{28,36},{32,40... | collective-permute-start | bytes 1572872 | tf_op jit(solution)/shard_map/ppermute | solution.py:9
  15.0 25.2 %collective-permute-start.1 = (bf16[1024,256]{1,0:T(8,128)(2,1)}, bf16[1024,256]{1,0:T(8,128)(2,1)}, u32[]{:S(2)}, u32[]{:S(2)}) collective-permute-start(bf16[1024,256]{1,0:T(8,128)(2,1)} %convolution_convert_fusion.1), channel_id=1, source_target_pairs={{0,4},{4,8},{8,12},{12,16},{16,20},{20,24},{24,28},{28,32},{32,36}... | collective-permute-start | bytes 1572872 | tf_op jit(solution)/shard_map/ppermute | solution.py:9
  19.9 23.7 %collective-permute-start.2 = (bf16[1024,256]{1,0:T(8,128)(2,1)}, bf16[1024,256]{1,0:T(8,128)(2,1)}, u32[]{:S(2)}, u32[]{:S(2)}) collective-permute-start(bf16[1024,256]{1,0:T(8,128)(2,1)} %convolution_convert_fusion.1), channel_id=1, source_target_pairs={{0,508},{4,0},{8,4},{12,8},{16,12},{20,16},{24,20},{28,24},{32,28}... | collective-permute-start | bytes 1572872 | tf_op jit(solution)/shard_map/ppermute | solution.py:9
  22.8 24.1 %collective-permute-start.3 = (bf16[1024,256]{1,0:T(8,128)(2,1)}, bf16[1024,256]{1,0:T(8,128)(2,1)}, u32[]{:S(2)}, u32[]{:S(2)}) collective-permute-start(bf16[1024,256]{1,0:T(8,128)(2,1)} %convolution_convert_fusion.1), channel_id=1, source_target_pairs={{0,504},{4,508},{8,0},{12,4},{16,8},{20,12},{24,16},{28,20},{32,24... | collective-permute-start | bytes 1572872 | tf_op jit(solution)/shard_map/ppermute | solution.py:9
  32.9 2.0 copy-start.12
  50.3 1.9 copy-start.6
  52.2 1.2 copy-start.3
  53.5 1.2 copy-start.7
  54.7 1.2 copy-start.9
  56.5 71.5 %copy-start.10 = (bf16[1024,256]{1,0:T(8,128)(2,1)S(1)}, bf16[1024,256]{1,0:T(8,128)(2,1)}, u32[]{:S(2)}) copy-start(bf16[1024,256]{1,0:T(8,128)(2,1)} %param.8) | copy-start | bytes 1572868
  57.8 1133.7 %all-reduce.6.cloned.1.call-start = ((), (), s32[]{:S(2)}) async-start(), calls=%async_computation.1 | async-start | bytes 524288 | tf_op jit(solution)/shard_map/psum | solution.py:74
  130.5 19.7 %collective-permute-start.4 = (bf16[1024,256]{1,0:T(8,128)(2,1)S(1)}, bf16[1024,256]{1,0:T(8,128)(2,1)}, u32[]{:S(2)}, u32[]{:S(2)}) collective-permute-start(bf16[1024,256]{1,0:T(8,128)(2,1)S(1)} %get-tuple-element.9), channel_id=1, source_target_pairs={{0,8},{4,12},{8,16},{12,20},{16,24},{20,28},{24,32},{28,36},{32,40... | collective-permute-start | bytes 1572872 | tf_op jit(solution)/shard_map/ppermute | solution.py:9
  132.6 22.8 %collective-permute-start.5 = (bf16[1024,256]{1,0:T(8,128)(2,1)S(1)}, bf16[1024,256]{1,0:T(8,128)(2,1)}, u32[]{:S(2)}, u32[]{:S(2)}) collective-permute-start(bf16[1024,256]{1,0:T(8,128)(2,1)S(1)} %get-tuple-element.9), channel_id=1, source_target_pairs={{0,4},{4,8},{8,12},{12,16},{16,20},{20,24},{24,28},{28,32},{32,36}... | collective-permute-start | bytes 1572872 | tf_op jit(solution)/shard_map/ppermute | solution.py:9
  137.7 22.9 %collective-permute-start.6 = (bf16[1024,256]{1,0:T(8,128)(2,1)S(1)}, bf16[1024,256]{1,0:T(8,128)(2,1)}, u32[]{:S(2)}, u32[]{:S(2)}) collective-permute-start(bf16[1024,256]{1,0:T(8,128)(2,1)S(1)} %get-tuple-element.9), channel_id=1, source_target_pairs={{0,508},{4,0},{8,4},{12,8},{16,12},{20,16},{24,20},{28,24},{32,28}... | collective-permute-start | bytes 1572872 | tf_op jit(solution)/shard_map/ppermute | solution.py:9
  139.6 29.0 %collective-permute-start.7 = (bf16[1024,256]{1,0:T(8,128)(2,1)S(1)}, bf16[1024,256]{1,0:T(8,128)(2,1)}, u32[]{:S(2)}, u32[]{:S(2)}) collective-permute-start(bf16[1024,256]{1,0:T(8,128)(2,1)S(1)} %get-tuple-element.9), channel_id=1, source_target_pairs={{0,504},{4,508},{8,0},{12,4},{16,8},{20,12},{24,16},{28,20},{32,24... | collective-permute-start | bytes 1572872 | tf_op jit(solution)/shard_map/ppermute | solution.py:9
  170.6 1.4 copy-start.4
  172.0 1.9 copy-start.2
  173.9 1.2 copy-start.5
  175.1 1.2 copy-start.8
  177.3 43.0 %copy-start.11 = (bf16[256,256]{1,0:T(8,128)(2,1)S(1)}, bf16[256,256]{1,0:T(8,128)(2,1)}, u32[]{:S(2)}) copy-start(bf16[256,256]{1,0:T(8,128)(2,1)} %param.7) | copy-start | bytes 393220
Sparse Core Ops, SparseCore 0:
  58.0 70.0 all-reduce.3
  220.4 971.0 all-reduce.5
where the time goes:
time: 1200 us
  waiting for transfers between devices  1040 us (87%)
  blocking collectives  41.9 us (3%)
  local copies, waits for them, and re-layouts  40.5 us (3%)
  starting transfers between devices  36.7 us (3%)
  matrix products  22.6 us (2%)
  between operations  14.4 us (1%)
    psum x1, waiting for transfers between devices, per_device(): weight_grad = lax.psum(grad_terms, 'rows')  970 us
    psum x1, waiting for transfers between devices, per_device(): aggregated = lax.psum(agg_part, 'rep')  70.2 us
    psum x1, blocking collectives, per_device(): back_sum = lax.psum(back_part, 'rep').astype(jnp.bfloat16)  41.9 us
    ppermute x8, starting transfers between devices, shifted(): return lax.ppermute(x, axis, [(i, (i + by) % size) for i in range(size)])  36.6 us
  transfers between devices with their start and end apart: 10, of which 3 were waited for; matrix products, arithmetic and copies ran while one was open for 3% of the time, Pallas kernels for 0%

commit v1 on v0

v1 whole, which is shorter than its diff:
```python
import functools

import jax
import jax.numpy as jnp
from jax import lax
from jax.experimental import pallas as pl
from jax.experimental.pallas import tpu as pltpu
from jax.sharding import PartitionSpec as P

MESH = pl.DeviceIdType.MESH
BF16 = jnp.bfloat16
F32 = jnp.float32


def matmul(a, b):
    return jnp.dot(a, b, preferred_element_type=F32)


def layer_kernel(
    groups,
    reps,
    scale,
    x_hbm,
    w_ref,
    ct_hbm,
    tiles_hbm,
    coords_ref,
    counts_ref,
    act_hbm,
    ig_hbm,
    wg_ref,
    px,
    ad,
    dense,
    tl,
    tp,
    code,
    acc,
    send,
    ra,
    cb,
    rf,
    g,
    ctv,
    actv,
    xt,
    load_sem,
    out_sem,
    x_send,
    x_recv,
    a_send,
    a_recv,
    rs_send,
    rs_recv,
    ag_send,
    ag_recv,
):
    me = lax.axis_index("rows")
    p = lax.axis_index("rep")
    up, dn = lax.rem(me + 2, groups), lax.rem(me + groups - 2, groups)
    odd = lax.rem(me, 2)
    mate = me + 1 - 2 * odd
    nxt, prv, opp = (lax.rem(p + k, reps) for k in (1, reps - 1, 2))
    n, f = acc.shape
    q = n // reps
    h = q // 2
    reach, slots, tile, _ = tl.shape
    blocks = n // tile
    out_slot = 1 + 2 * odd
    mate_slot = 3 - 2 * odd
    fwd_slot = 4 - 4 * odd
    far_slot = 4 * odd

    def rows(start, size):
        return pl.ds(pl.multiple_of(start, h), size)

    def remote(src, dst, ssem, rsem, dev):
        return pltpu.make_async_remote_copy(
            src_ref=src, dst_ref=dst, send_sem=ssem, recv_sem=rsem, device_id=dev, device_id_type=MESH
        )

    barrier = pltpu.get_barrier_semaphore()
    for dev in ((up, p), (dn, p), (mate, p), (me, nxt), (me, prv)):
        pl.semaphore_signal(barrier, inc=1, device_id=dev, device_id_type=MESH)

    loads = [
        pltpu.make_async_copy(src, dst, load_sem.at[i])
        for i, (src, dst) in enumerate(((tiles_hbm, tl), (x_hbm, px.at[2]), (ct_hbm, ctv)))
    ]
    for load in loads:
        load.start()

    pl.semaphore_wait(barrier, 5)

    def panel_copy(src, dst, ssem, rsem, kind, chunk):
        part = rows(chunk * q, q)
        slot = (0, 4, out_slot, mate_slot)[kind]
        dev = ((up, p), (dn, p), (mate, p), (mate, p))[kind]
        source = dst.at[fwd_slot, part] if kind == 3 else src.at[part]
        return remote(source, dst.at[slot, part], ssem.at[kind, chunk], rsem.at[slot, chunk], dev)

    def panel_wait(dst, ssem, rsem, slot, chunk):
        part = dst.at[slot, rows(chunk * q, q)]
        remote(part, part, ssem.at[0, chunk], rsem.at[slot, chunk], (mate, p)).wait_recv()

    @pl.loop(0, reps)
    def _(i):
        for kind in range(3):
            panel_copy(x_hbm, px, x_send, x_recv, kind, i).start()

    first = p * slots

    @pl.loop(0, reach)
    def _(d):
        for k in range(slots):
            live = first + k < counts_ref[0, d]
            at = coords_ref[0, 0, d, k] * blocks + coords_ref[1, 0, d, k]
            code[d * slots + k] = jnp.where(live, at, -1)

    tp[reach * slots] = jnp.zeros((tile, tile), BF16)
    loads[0].wait()

    @pl.loop(0, reach * slots)
    def _(t):
        base = (t // slots) * slots
        mine = code[t]
        total = jnp.zeros((tile, tile), F32)
        for j in range(slots):
            same = jnp.where(code[base + j] == mine, 1.0, 0.0).astype(F32)
            total = total + same * tl[t // slots, j].astype(F32)
        tp[t] = total.astype(BF16)

    @pl.loop(0, reach * blocks)
    def _(t):
        d = t // blocks
        b = lax.rem(t, blocks)
        part = pl.ds(pl.multiple_of(b * tile, tile), tile)
        for c in range(blocks):
            found = jnp.int32(reach * slots)
            for k in range(slots):
                found = jnp.where(code[d * slots + k] == b * blocks + c, d * slots + k, found)
            width = q // tile
            dense[d, c // width, part, (c % width) * tile : (c % width + 1) * tile] = tp[found]

    loads[1].wait()
    w = w_ref[...]

    def absorb(slot, chunk, panel, init=False):
        @pl.loop(0, reps)
        def _(b):
            part = rows(b * q, q)
            term = matmul(dense[slot, chunk, part, :], panel)
            acc[part, :] = term if init else acc[part, :] + term

    def x_absorb(slot, chunk, init=False):
        absorb(slot, chunk, matmul(px[slot, rows(chunk * q, q), :], w).astype(BF16), init)

    x_absorb(2, 0, True)

    @pl.loop(1, reps)
    def _(i):
        x_absorb(2, i)

    @pl.loop(0, reps)
    def _(i):
        xt[:, rows(i * q, q)] = px[2, rows(i * q, q), :].T

    @pl.loop(0, reps)
    def _(i):
        panel_wait(px, x_send, x_recv, mate_slot, i)
        x_absorb(mate_slot, i)

    @pl.loop(0, reps)
    def _(i):
        panel_wait(px, x_send, x_recv, fwd_slot, i)
        panel_copy(x_hbm, px, x_send, x_recv, 3, i).start()
        x_absorb(fwd_slot, i)
        panel_wait(px, x_send, x_recv, far_slot, i)
        x_absorb(far_slot, i)
        panel_wait(px, x_send, x_recv, out_slot, i)
        x_absorb(out_slot, i)

    sent = []

    def go(copy):
        copy.start()
        sent.append(copy)
        return copy

    def rs_start(ph):
        ssem, rsem = rs_send.at[ph], rs_recv.at[ph]
        buf = send.at[ph]

        def cast(part):
            buf[part, :] = acc[part, :].astype(BF16)

        cast(rows(opp * q, q))
        first_hop = [
            go(remote(buf.at[rows(opp * q, h)], ra.at[ph, 0], ssem.at[0], rsem.at[0], (me, nxt))),
            go(remote(buf.at[rows(opp * q + h, h)], ra.at[ph, 1], ssem.at[1], rsem.at[1], (me, prv))),
        ]
        cast(rows(nxt * q, q))
        cast(rows(prv * q, q))
        last_hop = [
            go(remote(buf.at[rows(nxt * q + h, h)], rf.at[ph, 0, pl.ds(h, h)], ssem.at[2], rsem.at[2], (me, nxt))),
            go(remote(buf.at[rows(prv * q, h)], rf.at[ph, 1, pl.ds(0, h)], ssem.at[3], rsem.at[3], (me, prv))),
        ]
        return first_hop, last_hop

    def rs_finish(ph, copies):
        ssem, rsem = rs_send.at[ph], rs_recv.at[ph]
        first_hop, last_hop = copies
        for k, (start, dev) in enumerate(((nxt * q, nxt), (prv * q + h, prv))):
            first_hop[k].wait_recv()
            cb[ph, k] = (ra[ph, k].astype(F32) + acc[rows(start, h), :]).astype(BF16)
            last_hop.append(
                go(remote(cb.at[ph, k], rf.at[ph, k, pl.ds(k * h, h)], ssem.at[4 + k], rsem.at[4 + k], (me, dev)))
            )
        for copy in last_hop:
            copy.wait_recv()
        return acc[rows(p * q, q), :] + rf[ph, 0].astype(F32) + rf[ph, 1].astype(F32)

    def ag_copy(ph, k, start, size, dev):
        part = g.at[ph, rows(start, size)]
        return remote(part, part, ag_send.at[ph, k], ag_recv.at[ph, k], (me, dev))

    def ag_start(ph):
        go(ag_copy(ph, 0, p * q, q, nxt))
        go(ag_copy(ph, 1, p * q, q, prv))

    def ag_pass(ph, k):
        if k == 0:
            ag_copy(ph, 0, prv * q, q, prv).wait_recv()
            go(ag_copy(ph, 2, prv * q, h, nxt))
        else:
            ag_copy(ph, 1, nxt * q, q, nxt).wait_recv()
            go(ag_copy(ph, 3, nxt * q + h, h, prv))

    def ag_last(ph):
        ag_copy(ph, 2, opp * q, h, prv).wait_recv()
        ag_copy(ph, 3, opp * q + h, h, nxt).wait_recv()

    def store_out(k, src, dst, start, size):
        part = rows(start, size)
        copy = pltpu.make_async_copy(src.at[part], dst.at[part], out_sem.at[k])
        copy.start()
        return copy

    outs = []

    g[0, rows(p * q, q), :] = rs_finish(0, rs_start(0)).astype(BF16)
    ag_start(0)
    loads[2].wait()

    def activate(k, at):
        part = rows(at * q, q)
        value = g[0, part, :].astype(F32)
        sig = jax.nn.sigmoid(value)
        ad[2, part, :] = (ctv[part, :].astype(F32) * (sig * (1.0 + value * (1.0 - sig)))).astype(BF16)
        for kind in range(3):
            panel_copy(ad.at[2], ad, a_send, a_recv, kind, at).start()
        actv[part, :] = (value * sig).astype(BF16)
        outs.append(store_out(k, actv, act_hbm, at * q, q))

    def a_absorb(slot, chunk, init=False):
        absorb(slot, chunk, ad[slot, rows(chunk * q, q), :], init)

    def a_round(at):
        panel_wait(ad, a_send, a_recv, fwd_slot, at)
        panel_copy(ad.at[2], ad, a_send, a_recv, 3, at).start()
        panel_wait(ad, a_send, a_recv, mate_slot, at)
        a_absorb(mate_slot, at)
        a_absorb(fwd_slot, at)
        panel_wait(ad, a_send, a_recv, far_slot, at)
        a_absorb(far_slot, at)
        panel_wait(ad, a_send, a_recv, out_slot, at)
        a_absorb(out_slot, at)

    activate(0, p)
    a_absorb(2, p, True)
    ag_pass(0, 0)
    activate(1, prv)
    ag_pass(0, 1)
    activate(2, nxt)
    a_absorb(2, prv)
    a_round(p)
    ag_last(0)
    activate(3, opp)
    a_absorb(2, nxt)
    a_absorb(2, opp)

    @pl.loop(0, reps - 1)
    def _(j):
        a_round(jnp.where(j == 0, prv, jnp.where(j == 1, nxt, opp)))

    copies = rs_start(1)
    send[1, rows(p * q, q), :] = acc[rows(p * q, q), :].astype(BF16)
    wg_ref[...] = matmul(xt[...], send[1]) * scale
    back = rs_finish(1, copies).astype(BF16)
    g[1, rows(p * q, q), :] = lax.dot_general(
        back, w, (((1,), (1,)), ((), ())), preferred_element_type=F32
    ).astype(BF16)
    ag_start(1)
    outs.append(store_out(4, g.at[1], ig_hbm, p * q, q))
    ag_pass(1, 0)
    outs.append(store_out(5, g.at[1], ig_hbm, prv * q, q))
    ag_pass(1, 1)
    outs.append(store_out(6, g.at[1], ig_hbm, nxt * q, q))
    ag_last(1)
    outs.append(store_out(7, g.at[1], ig_hbm, opp * q, q))

    for copy in sent:
        copy.wait_send()

    @pl.loop(0, reps)
    def _(i):
        for kind in range(4):
            panel_copy(x_hbm, px, x_send, x_recv, kind, i).wait_send()
            panel_copy(ad.at[2], ad, a_send, a_recv, kind, i).wait_send()

    for copy in outs:
        copy.wait()


def per_device(groups, reps, node_feats, weight, cotangent, tile_values, tile_coords, tile_counts):
    n, f = node_feats.shape
    _, reach, slots, tile, _ = tile_values.shape
    q = n // reps
    h = q // 2
    dma = pltpu.SemaphoreType.DMA
    hbm = pl.BlockSpec(memory_space=pl.ANY)
    vmem = pl.BlockSpec(memory_space=pltpu.VMEM)
    smem = pl.BlockSpec(memory_space=pltpu.SMEM)
    activated, input_grad, grad_terms = pl.pallas_call(
        functools.partial(layer_kernel, groups, reps, (n * groups) ** (-0.5)),
        out_shape=(
            jax.ShapeDtypeStruct((n, f), BF16),
            jax.ShapeDtypeStruct((n, f), BF16),
            jax.ShapeDtypeStruct((f, f), F32),
        ),
        in_specs=[hbm, vmem, hbm, hbm, smem, smem],
        out_specs=(hbm, hbm, vmem),
        scratch_shapes=[
            pltpu.VMEM((reach, n, f), BF16),
            pltpu.VMEM((reach, n, f), BF16),
            pltpu.VMEM((reach, reps, n, q), BF16),
            pltpu.VMEM((reach, slots, tile, tile), BF16),
            pltpu.VMEM((reach * slots + 1, tile, tile), BF16),
            pltpu.SMEM((reach * slots,), jnp.int32),
            pltpu.VMEM((n, f), F32),
            pltpu.VMEM((2, n, f), BF16),
            pltpu.VMEM((2, 2, h, f), BF16),
            pltpu.VMEM((2, 2, h, f), BF16),
            pltpu.VMEM((2, 2, q, f), BF16),
            pltpu.VMEM((2, n, f), BF16),
            pltpu.VMEM((n, f), BF16),
            pltpu.VMEM((n, f), BF16),
            pltpu.VMEM((f, n), BF16),
            dma((3,)),
            dma((8,)),
            dma((4, reps)),
            dma((reach, reps)),
            dma((4, reps)),
            dma((reach, reps)),
            dma((2, 6)),
            dma((2, 6)),
            dma((2, 4)),
            dma((2, 4)),
        ],
        compiler_params=pltpu.CompilerParams(
            collective_id=0, has_side_effects=True, vmem_limit_bytes=56 << 20
        ),
    )(node_feats, weight, cotangent, tile_values[0], tile_coords, tile_counts)
    weight_grad = lax.psum(grad_terms, ("rows", "rep"))
    return (activated, input_grad, weight_grad)


def solution(mesh):
    return jax.shard_map(
        functools.partial(per_device, mesh.shape["rows"], mesh.shape["rep"]),
        mesh=mesh,
        in_specs=(
            P("rows", None),
            P(),
            P("rows", None),
            P("rows", None, "rep", None, None),
            P(None, "rows", None, "rep"),
            P("rows", None),
        ),
        out_specs=(P("rows", None), P("rows", None), P()),
        check_vma=False,
    )
```

time: 1200 us -> 394 us (0.33)
  waiting for transfers between devices: 1040 us -> 276 us
  Pallas kernels: 0 us -> 98.4 us
  blocking collectives: 41.9 us -> 0 us
  starting transfers between devices: 36.7 us -> 0.04 us
  local copies, waits for them, and re-layouts: 40.5 us -> 4.71 us
  matrix products: 22.6 us -> 0 us
    psum x2 -> x1, waiting for transfers between devices: 1040 us -> 276 us  [per_device(): weight_grad = lax.psum(grad_terms, ('rows', 'rep'))]
    pallas_call x0 -> x1, Pallas kernels: none -> 98.4 us  [per_device(): pl.pallas_call(functools.partial(layer_kernel, groups, reps, (n * groups)...]
    psum x1 -> x0, blocking collectives: 41.9 us -> none  [per_device(): back_sum = lax.psum(back_part, 'rep').astype(jnp.bfloat16)]
    ppermute x8 -> x0, starting transfers between devices: 36.6 us -> none  [shifted(): return lax.ppermute(x, axis, [(i, (i + by) % size) for i in range(size)])]
    dot_general x23 -> x0, matrix products: 22.6 us -> none  [the longest x10 10.8 us: offset_terms(): jnp.einsum('kb,kuf->buf', place, product, precision=lax.Precision.HIGHEST)]
    gather x10 -> x0, local copies, waits for them, and re-layouts: 18.3 us -> none  [offset_terms(): picked = panel[cols_idx]]
    dot_general x10 -> x0, local copies, waits for them, and re-layouts: 13.9 us -> none  [offset_terms(): jnp.einsum('kuv,kvf->kuf', values, picked, preferred_element_type=jnp.flo...]
  transfers between devices with their start and end apart: 10 -> 1, of which waited for: 3 -> 1; matrix products, arithmetic and copies ran while one was open for 3% -> 0% of each run, Pallas kernels for 0% -> 0%
where the time goes in v1:
time: 394 us; the launch traced here: 393 us
  waiting for transfers between devices  276 us (70%)
  Pallas kernels  98.4 us (25%)
  between operations  14 us (4%)
  local copies, waits for them, and re-layouts  4.71 us (1%)
    psum x1, waiting for transfers between devices, per_device(): weight_grad = lax.psum(grad_terms, ('rows', 'rep'))  276 us
    pallas_call x1, Pallas kernels, per_device(): pl.pallas_call(functools.partial(layer_kernel, groups, reps, (n * groups)...  98.4 us
  transfers between devices with their start and end apart: 1, of which 1 were waited for; matrix products, arithmetic and copies ran while one was open for 0% of the time, Pallas kernels for 0%

profile of v1, /device:TPU:1, one launch (start us, length us, event | category | flops | bytes accessed | tf_op | source)
XLA Modules:
  0.0 393.3 jit_solution(16682474259295444244)
XLA Ops:
  7.2 0.0 all-reduce.2.cloned.1.call-start
  7.2 1.3 copy.9.coords_ref
  8.5 98.4 %shard_map.85 = (bf16[1024,256]{1,0:T(8,128)(2,1)}, bf16[1024,256]{1,0:T(8,128)(2,1)}, f32[256,256]{1,0:T(8,128)}) custom-call(bf16[1024,256]{1,0:T(8,128)(2,1)} %x_hbm.1, bf16[256,256]{1,0:T(8,128)(2,1)} %w_ref.1, bf16[1024,256]{1,0:T(8,128)(2,1)} %ct_hbm.1, bf16[5,8,128,128]{3,2,1,0:T(8,128)(2,1)} %bitcast.1, s32[2,1,5,8]{3,2,1,0:T(8,128)} %copy.9.coords_ref, ...), custom_call_target="tpu_custom_call" | custom-call | tf_op jit(solution)/shard_map/pallas_call | solution.py:334
  106.9 0.0 copy-start
  106.9 0.0 all-reduce.2.cloned.1.call-update
  106.9 276.1 %all-reduce.2.cloned.1.call-done = f32[256,256]{1,0:T(8,128)} async-done(((f32[256,256]{1,0:T(8,128)}), f32[256,256]{1,0:T(8,128)}) %all-reduce.2.cloned.1.call-update) | async-done | bytes 262160 | tf_op jit(solution)/shard_map/psum | solution.py:374
  383.0 0.0 copy-start.1
  383.0 1.9 copy.14
  384.9 0.0 copy-done
  384.9 0.8 copy.15
  385.7 0.0 copy-done.1
  385.7 0.7 copy.16
Async XLA Ops:
  7.2 375.9 %all-reduce.2.cloned.1.call-start = ((), (), s32[]{:S(2)}) async-start(), calls=%async_computation | async-start | bytes 524288 | tf_op jit(solution)/shard_map/psum | solution.py:374
  106.9 278.1 %copy-start = (bf16[1024,256]{1,0:T(8,128)(2,1)S(1)}, bf16[1024,256]{1,0:T(8,128)(2,1)}, u32[]{:S(2)}) copy-start(bf16[1024,256]{1,0:T(8,128)(2,1)} %get-tuple-element.13) | copy-start | bytes 1572868
  383.0 2.7 copy-start.1
Sparse Core Ops, SparseCore 0:
  107.0 275.9 all-reduce.1

commit v2 on v1

v2 whole, which is shorter than its diff:
```python
import functools

import jax
import jax.numpy as jnp
from jax import lax
from jax.experimental import pallas as pl
from jax.experimental.pallas import tpu as pltpu
from jax.sharding import PartitionSpec as P

MESH = pl.DeviceIdType.MESH
BF16 = jnp.bfloat16
F32 = jnp.float32
ZS, XS, YL = 8, 4, 2


def matmul(a, b):
    return jnp.dot(a, b, preferred_element_type=F32)


def layer_kernel(
    groups,
    reps,
    scale,
    x_hbm,
    w_ref,
    ct_hbm,
    tiles_hbm,
    coords_ref,
    counts_ref,
    act_hbm,
    ig_hbm,
    wg_hbm,
    px,
    ad,
    dense,
    tl,
    tp,
    code,
    acc,
    send,
    ra,
    cb,
    rf,
    g,
    ctv,
    actv,
    v,
    xt,
    ws,
    w0,
    w1s,
    w1,
    w2,
    w3,
    wf,
    wp,
    w1f,
    load_sem,
    out_sem,
    x_send,
    x_recv,
    a_send,
    a_recv,
    rs_send,
    rs_recv,
    ag_send,
    ag_recv,
    w_send,
    w_recv,
):
    me = lax.axis_index("rows")
    p = lax.axis_index("rep")
    up, dn = lax.rem(me + 2, groups), lax.rem(me + groups - 2, groups)
    odd = lax.rem(me, 2)
    mate = me + 1 - 2 * odd
    nxt, prv, opp = (lax.rem(p + k, reps) for k in (1, reps - 1, 2))
    n, f = acc.shape
    q = n // reps
    h = q // 2
    reach, slots, tile, _ = tl.shape
    blocks = n // tile
    out_slot = 1 + 2 * odd
    mate_slot = 3 - 2 * odd
    fwd_slot = 4 - 4 * odd
    far_slot = 4 * odd

    def rows(start, size):
        return pl.ds(pl.multiple_of(start, h), size)

    def remote(src, dst, ssem, rsem, dev):
        return pltpu.make_async_remote_copy(
            src_ref=src, dst_ref=dst, send_sem=ssem, recv_sem=rsem, device_id=dev, device_id_type=MESH
        )

    z = lax.rem(me // 2, ZS)
    x = lax.rem(me // (2 * ZS), XS)
    y_lo = me // (2 * ZS * XS)
    y = p * YL + y_lo

    def z_peer(k):
        other = lax.rem(z + k, ZS)
        return other, (me + 2 * (other - z), p)

    def x_peer(k):
        other = lax.rem(x + k, XS)
        return other, (me + 2 * ZS * (other - x), p)

    def y_peer(k):
        other = lax.rem(y + k, YL * reps)
        return other, (me + 2 * ZS * XS * (lax.rem(other, YL) - y_lo), other // YL)

    z_peers = [z_peer(k) for k in range(1, ZS)]
    x_peers = [x_peer(k) for k in range(1, XS)]
    y_peers = [y_peer(k) for k in range(1, YL * reps)]
    greet = [(up, p), (dn, p), (mate, p)] + [dev for _, dev in z_peers + x_peers + y_peers]

    barrier = pltpu.get_barrier_semaphore()
    for dev in greet:
        pl.semaphore_signal(barrier, inc=1, device_id=dev, device_id_type=MESH)

    loads = [
        pltpu.make_async_copy(src, dst, load_sem.at[i])
        for i, (src, dst) in enumerate(((tiles_hbm, tl), (x_hbm, px.at[2]), (ct_hbm, ctv)))
    ]
    for load in loads:
        load.start()

    pl.semaphore_wait(barrier, len(greet))

    def panel_copy(src, dst, ssem, rsem, kind, chunk, size):
        part = rows(chunk * size, size)
        slot = (0, 4, out_slot, mate_slot)[kind]
        dev = ((up, p), (dn, p), (mate, p), (mate, p))[kind]
        source = dst.at[fwd_slot, part] if kind == 3 else src.at[part]
        return remote(source, dst.at[slot, part], ssem.at[kind, chunk], rsem.at[slot, chunk], dev)

    def panel_wait(dst, ssem, rsem, slot, chunk, size):
        part = dst.at[slot, rows(chunk * size, size)]
        remote(part, part, ssem.at[0, chunk], rsem.at[slot, chunk], (mate, p)).wait_recv()

    def x_copy(kind, chunk):
        return panel_copy(x_hbm, px, x_send, x_recv, kind, chunk, q)

    def x_wait(slot, chunk):
        panel_wait(px, x_send, x_recv, slot, chunk, q)

    def a_copy(kind, chunk):
        return panel_copy(ad.at[2], ad, a_send, a_recv, kind, chunk, h)

    def a_wait(slot, at):
        panel_wait(ad, a_send, a_recv, slot, 2 * at, h)
        panel_wait(ad, a_send, a_recv, slot, 2 * at + 1, h)

    def x_forward(chunk):
        x_wait(fwd_slot, chunk)
        x_copy(3, chunk).start()

    def a_forward(chunk):
        panel_wait(ad, a_send, a_recv, fwd_slot, chunk, h)
        a_copy(3, chunk).start()

    @pl.loop(0, reps)
    def _(i):
        for kind in range(3):
            x_copy(kind, i).start()

    first = p * slots

    @pl.loop(0, reach)
    def _(d):
        for k in range(slots):
            live = first + k < counts_ref[0, d]
            at = coords_ref[0, 0, d, k] * blocks + coords_ref[1, 0, d, k]
            code[d * slots + k] = jnp.where(live, at, -1)

    tp[reach * slots] = jnp.zeros((tile, tile), BF16)
    loads[0].wait()

    @pl.loop(0, reach)
    def _(d):
        for k in range(slots):
            total = tl[d, k].astype(F32)
            for j in range(k + 1, slots):
                same = jnp.where(code[d * slots + j] == code[d * slots + k], 1.0, 0.0).astype(F32)
                total = total + same * tl[d, j].astype(F32)
            tp[d * slots + k] = total.astype(BF16)

    @pl.loop(0, reach * blocks)
    def _(t):
        d = t // blocks
        b = lax.rem(t, blocks)
        part = pl.ds(pl.multiple_of(b * tile, tile), tile)
        for c in range(blocks):
            found = jnp.int32(reach * slots)
            for k in range(slots - 1, -1, -1):
                found = jnp.where(code[d * slots + k] == b * blocks + c, d * slots + k, found)
            width = q // tile
            dense[d, c // width, part, (c % width) * tile : (c % width + 1) * tile] = tp[found]

    loads[1].wait()
    w = w_ref[...]

    sent = []

    def go(copy):
        copy.start()
        sent.append(copy)
        return copy

    def absorb(slot, chunk, panel, init=False):
        term = matmul(dense[slot, chunk], panel)
        acc[...] = term if init else acc[...] + term

    def x_panel(slot, chunk):
        return matmul(px[slot, rows(chunk * q, q), :], w).astype(BF16)

    def x_whole(slot, init=False):
        for i in range(reps):
            v[pl.ds(i * q, q), :] = x_panel(slot, i)
        total = None if init else acc[...]
        for i in range(reps):
            term = matmul(dense[slot, i], v[pl.ds(i * q, q), :])
            total = term if total is None else total + term
        acc[...] = total

    def rs_start(ph, chunk, panels):
        ssem, rsem = rs_send.at[ph], rs_recv.at[ph]
        buf = send.at[ph]

        def block(at):
            part = rows(at * q, q)
            total = acc[part, :]
            for slot, panel in panels:
                total = total + matmul(dense[slot, chunk, part, :], panel())
            acc[part, :] = total
            buf[part, :] = total.astype(BF16)

        block(opp)
        first_hop = [
            go(remote(buf.at[rows(opp * q, h)], ra.at[ph, 0], ssem.at[0], rsem.at[0], (me, nxt))),
            go(remote(buf.at[rows(opp * q + h, h)], ra.at[ph, 1], ssem.at[1], rsem.at[1], (me, prv))),
        ]
        block(nxt)
        last_hop = [
            go(remote(buf.at[rows(nxt * q + h, h)], rf.at[ph, 0, pl.ds(h, h)], ssem.at[2], rsem.at[2], (me, nxt))),
        ]
        block(prv)
        last_hop.append(
            go(remote(buf.at[rows(prv * q, h)], rf.at[ph, 1, pl.ds(0, h)], ssem.at[3], rsem.at[3], (me, prv)))
        )
        block(p)
        return first_hop, last_hop

    x_whole(2, True)
    x_forward(0)

    @pl.loop(0, reps)
    def _(i):
        x_wait(mate_slot, i)

    x_whole(mate_slot)

    @pl.loop(0, reps)
    def _(i):
        xt[:, rows(i * q, q)] = px[2, rows(i * q, q), :].T

    @pl.loop(0, reps - 1)
    def _(i):
        absorb(fwd_slot, i, x_panel(fwd_slot, i))
        x_wait(far_slot, i)
        absorb(far_slot, i, x_panel(far_slot, i))
        x_forward(i + 1)
        x_wait(out_slot, i)
        absorb(out_slot, i, x_panel(out_slot, i))

    last = reps - 1
    v[pl.ds(0, q), :] = x_panel(fwd_slot, last)
    x_wait(far_slot, last)
    v[pl.ds(q, q), :] = x_panel(far_slot, last)
    x_wait(out_slot, last)
    v[pl.ds(2 * q, q), :] = x_panel(out_slot, last)
    x_last = [
        (fwd_slot, lambda: v[pl.ds(0, q), :]),
        (far_slot, lambda: v[pl.ds(q, q), :]),
        (out_slot, lambda: v[pl.ds(2 * q, q), :]),
    ]

    def rs_middle(ph, copies):
        ssem, rsem = rs_send.at[ph], rs_recv.at[ph]
        first_hop, last_hop = copies
        for k, (start, dev) in enumerate(((nxt * q, nxt), (prv * q + h, prv))):
            first_hop[k].wait_recv()
            cb[ph, k] = (ra[ph, k].astype(F32) + acc[rows(start, h), :]).astype(BF16)
            last_hop.append(
                go(remote(cb.at[ph, k], rf.at[ph, k, pl.ds(k * h, h)], ssem.at[4 + k], rsem.at[4 + k], (me, dev)))
            )
        return last_hop

    def rs_finish(ph, last_hop):
        for copy in last_hop:
            copy.wait_recv()
        return acc[rows(p * q, q), :] + rf[ph, 0].astype(F32) + rf[ph, 1].astype(F32)

    def ag_copy(ph, k, at, half, dev):
        part = g.at[ph, rows(at * q + half * h, h)]
        return remote(part, part, ag_send.at[ph, k], ag_recv.at[ph, k], (me, dev))

    def ag_start(ph):
        go(ag_copy(ph, 0, p, 0, nxt))
        go(ag_copy(ph, 1, p, 1, prv))
        go(ag_copy(ph, 2, p, 1, nxt))
        go(ag_copy(ph, 3, p, 0, prv))

    def ag_wait(ph, k):
        at, half = ((prv, 0), (nxt, 1), (prv, 1), (nxt, 0), (opp, 0), (opp, 1))[k]
        ag_copy(ph, k, at, half, prv).wait_recv()
        if k < 2:
            go(ag_copy(ph, 4 + k, at, half, (nxt, prv)[k]))

    def store_out(k, src, dst, start, size):
        part = rows(start, size)
        copy = pltpu.make_async_copy(src.at[part], dst.at[part], out_sem.at[k])
        copy.start()
        return copy

    outs = []

    g[0, rows(p * q, q), :] = rs_finish(0, rs_middle(0, rs_start(0, last, x_last))).astype(BF16)
    ag_start(0)
    loads[2].wait()

    def activate(at, half):
        start = at * q + half * h
        part = rows(start, h)
        value = g[0, part, :].astype(F32)
        sig = jax.nn.sigmoid(value)
        ad[2, part, :] = (ctv[part, :].astype(F32) * (sig * (1.0 + value * (1.0 - sig)))).astype(BF16)
        for kind in range(3):
            a_copy(kind, 2 * at + half).start()
        actv[part, :] = (value * sig).astype(BF16)
        outs.append(store_out(len(outs), actv, act_hbm, start, h))

    def a_panel(slot, chunk):
        return ad[slot, rows(chunk * q, q), :]

    activate(p, 0)
    activate(p, 1)
    absorb(2, p, a_panel(2, p), True)
    ag_wait(0, 0)
    activate(prv, 0)
    ag_wait(0, 1)
    activate(nxt, 1)
    a_forward(2 * p)
    a_forward(2 * p + 1)
    ag_wait(0, 2)
    activate(prv, 1)
    ag_wait(0, 3)
    activate(nxt, 0)
    a_wait(mate_slot, p)
    absorb(mate_slot, p, a_panel(mate_slot, p))
    absorb(fwd_slot, p, a_panel(fwd_slot, p))
    ag_wait(0, 4)
    activate(opp, 0)
    ag_wait(0, 5)
    activate(opp, 1)
    a_forward(2 * prv)
    a_forward(2 * nxt + 1)
    a_wait(far_slot, p)
    a_wait(out_slot, p)

    @pl.loop(0, 2)
    def _(i):
        slot = jnp.where(i == 0, far_slot, out_slot)
        absorb(slot, p, a_panel(slot, p))

    a_forward(2 * prv + 1)
    a_forward(2 * nxt)
    for at in (prv, nxt, opp):
        a_wait(mate_slot, at)

    @pl.loop(0, 6)
    def _(i):
        at = jnp.where(i // 2 == 0, prv, jnp.where(i // 2 == 1, nxt, opp))
        slot = jnp.where(lax.rem(i, 2) == 0, 2, mate_slot)
        absorb(slot, at, a_panel(slot, at))

    for at in (prv, nxt):
        a_wait(far_slot, at)
        a_wait(out_slot, at)

    @pl.loop(0, 6)
    def _(i):
        at = jnp.where(i < 3, prv, nxt)
        turn = lax.rem(i, 3)
        slot = jnp.where(turn == 0, fwd_slot, jnp.where(turn == 1, far_slot, out_slot))
        absorb(slot, at, a_panel(slot, at))

    a_forward(2 * opp)
    a_forward(2 * opp + 1)
    a_wait(far_slot, opp)
    a_wait(out_slot, opp)
    a_last = [(slot, functools.partial(a_panel, slot, opp)) for slot in (fwd_slot, far_slot, out_slot)]

    def w_go(step, to, src, dst, slot, dev):
        go(remote(src, dst, w_send.at[step, to], w_recv.at[step, slot], dev))

    def w_wait(step, ref, slot):
        remote(ref, ref, w_send.at[step, 0], w_recv.at[step, slot], (mate, p)).wait_recv()

    half, piece = f // 2, f // (2 * ZS)

    copies = rs_start(1, opp, a_last)
    terms = matmul(xt[...], send[1]) * scale
    wp[...] = terms
    ws[...] = terms.astype(BF16)
    w_go(0, 0, ws.at[rows((1 - odd) * half, half)], w0, 0, (mate, p))
    last_hop = rs_middle(1, copies)
    w_wait(0, w0, 0)
    mine = wp[rows(odd * half, half), :] + w0[...].astype(F32)
    w1f[...] = mine.reshape(ZS, piece, f)
    w1s[...] = w1f[...].astype(BF16)
    for other, dev in z_peers:
        w_go(1, other, w1s.at[other], w1.at[z], z, dev)
    part = w1f[z]
    for other, dev in z_peers:
        w_wait(1, w1.at[other], other)
        part = part + w1[other].astype(F32)
    w2[x] = part.astype(BF16)
    for other, dev in x_peers:
        w_go(2, other, w2.at[x], w2.at[x], x, dev)
    back = rs_finish(1, last_hop).astype(BF16)
    g[1, rows(p * q, q), :] = lax.dot_general(
        back, w, (((1,), (1,)), ((), ())), preferred_element_type=F32
    ).astype(BF16)
    ag_start(1)
    outs.append(store_out(len(outs), g.at[1], ig_hbm, p * q, q))
    for other, dev in x_peers:
        w_wait(2, w2.at[other], other)
    w3[y] = sum(w2[k].astype(F32) for k in range(XS)).astype(BF16)
    for other, dev in y_peers:
        w_go(3, other, w3.at[y], w3.at[y], y, dev)
    ag_wait(1, 0)
    ag_wait(1, 1)
    ag_wait(1, 2)
    outs.append(store_out(len(outs), g.at[1], ig_hbm, prv * q, q))
    ag_wait(1, 3)
    outs.append(store_out(len(outs), g.at[1], ig_hbm, nxt * q, q))
    for other, dev in y_peers:
        w_wait(3, w3.at[other], other)
    wf[odd, z] = sum(w3[k].astype(F32) for k in range(YL * reps))
    for other, dev in z_peers:
        w_go(4, other, wf.at[odd, z], wf.at[odd, z], z, dev)
    ag_wait(1, 4)
    ag_wait(1, 5)
    outs.append(store_out(len(outs), g.at[1], ig_hbm, opp * q, q))
    for other, dev in z_peers:
        w_wait(4, wf.at[odd, other], other)
    w_go(5, 0, wf.at[odd], wf.at[odd], 0, (mate, p))
    w_wait(5, wf.at[1 - odd], 0)
    copy = pltpu.make_async_copy(wf, wg_hbm, out_sem.at[len(outs)])
    copy.start()
    outs.append(copy)

    for copy in sent:
        copy.wait_send()

    @pl.loop(0, reps)
    def _(i):
        for kind in range(4):
            x_copy(kind, i).wait_send()

    @pl.loop(0, 2 * reps)
    def _(i):
        for kind in range(4):
            a_copy(kind, i).wait_send()

    for copy in outs:
        copy.wait()


def per_device(groups, reps, node_feats, weight, cotangent, tile_values, tile_coords, tile_counts):
    n, f = node_feats.shape
    _, reach, slots, tile, _ = tile_values.shape
    q = n // reps
    h = q // 2
    dma = pltpu.SemaphoreType.DMA
    piece = f // (2 * ZS)
    hbm = pl.BlockSpec(memory_space=pl.ANY)
    vmem = pl.BlockSpec(memory_space=pltpu.VMEM)
    smem = pl.BlockSpec(memory_space=pltpu.SMEM)
    activated, input_grad, weight_grad = pl.pallas_call(
        functools.partial(layer_kernel, groups, reps, (n * groups) ** (-0.5)),
        out_shape=(
            jax.ShapeDtypeStruct((n, f), BF16),
            jax.ShapeDtypeStruct((n, f), BF16),
            jax.ShapeDtypeStruct((2, ZS, piece, f), F32),
        ),
        in_specs=[hbm, vmem, hbm, hbm, smem, smem],
        out_specs=(hbm, hbm, hbm),
        scratch_shapes=[
            pltpu.VMEM((reach, n, f), BF16),
            pltpu.VMEM((reach, n, f), BF16),
            pltpu.VMEM((reach, reps, n, q), BF16),
            pltpu.VMEM((reach, slots, tile, tile), BF16),
            pltpu.VMEM((reach * slots + 1, tile, tile), BF16),
            pltpu.SMEM((reach * slots,), jnp.int32),
            pltpu.VMEM((n, f), F32),
            pltpu.VMEM((2, n, f), BF16),
            pltpu.VMEM((2, 2, h, f), BF16),
            pltpu.VMEM((2, 2, h, f), BF16),
            pltpu.VMEM((2, 2, q, f), BF16),
            pltpu.VMEM((2, n, f), BF16),
            pltpu.VMEM((n, f), BF16),
            pltpu.VMEM((n, f), BF16),
            pltpu.VMEM((n, f), BF16),
            pltpu.VMEM((f, n), BF16),
            pltpu.VMEM((f, f), BF16),
            pltpu.VMEM((f // 2, f), BF16),
            pltpu.VMEM((ZS, piece, f), BF16),
            pltpu.VMEM((ZS, piece, f), BF16),
            pltpu.VMEM((XS, piece, f), BF16),
            pltpu.VMEM((YL * reps, piece, f), BF16),
            pltpu.VMEM((2, ZS, piece, f), F32),
            pltpu.VMEM((f, f), F32),
            pltpu.VMEM((ZS, piece, f), F32),
            dma((3,)),
            dma((16,)),
            dma((4, reps)),
            dma((reach, reps)),
            dma((4, 2 * reps)),
            dma((reach, 2 * reps)),
            dma((2, 6)),
            dma((2, 6)),
            dma((2, 6)),
            dma((2, 6)),
            dma((6, 8)),
            dma((6, 8)),
        ],
        compiler_params=pltpu.CompilerParams(
            collective_id=0, vmem_limit_bytes=56 << 20
        ),
    )(node_feats, weight, cotangent, tile_values[0], tile_coords, tile_counts)
    return (activated, input_grad, weight_grad.reshape(f, f))


def solution(mesh):
    return jax.shard_map(
        functools.partial(per_device, mesh.shape["rows"], mesh.shape["rep"]),
        mesh=mesh,
        in_specs=(
            P("rows", None),
            P(),
            P("rows", None),
            P("rows", None, "rep", None, None),
            P(None, "rows", None, "rep"),
            P("rows", None),
        ),
        out_specs=(P("rows", None), P("rows", None), P()),
        check_vma=False,
    )
```

time: 394 us -> 107 us (0.27)
  waiting for transfers between devices: 276 us -> 0 us
  between operations: 14 us -> 0.66 us
    psum x1 -> x0, waiting for transfers between devices: 276 us -> none  [per_device(): weight_grad = lax.psum(grad_terms, ('rows', 'rep'))]
  transfers between devices with their start and end apart: 1 -> 0, of which waited for: 1 -> 0; matrix products, arithmetic and copies ran while one was open for 0% -> 0% of each run, Pallas kernels for 0% -> 0%
where the time goes in v2:
time: 107 us; the launch traced here: 105 us
  Pallas kernels  99.6 us (93%)
  local copies, waits for them, and re-layouts  4.74 us (4%)
    pallas_call x1, Pallas kernels, per_device(): pl.pallas_call(functools.partial(layer_kernel, groups, reps, (n * groups)...  99.6 us
    unnamed x8, local copies, waits for them, and re-layouts  4.74 us

profile of v2, /device:TPU:1, one launch (start us, length us, event | category | flops | bytes accessed | tf_op | source)
XLA Modules:
  0.0 105.0 jit_solution(1093299028859450247)
XLA Ops:
  0.6 1.3 %copy.9.coords_ref = s32[2,1,5,8]{3,2,1,0:T(8,128)} copy(s32[2,1,5,8]{3,1,2,0:T(1,128)} %param.10) | data formatting | bytes 640 | tf_op args[4]
  1.9 99.6 %shard_map.85 = (bf16[1024,256]{1,0:T(8,128)(2,1)}, bf16[1024,256]{1,0:T(8,128)(2,1)}, f32[2,8,16,256]{3,2,1,0:T(8,128)}) custom-call(bf16[1024,256]{1,0:T(8,128)(2,1)} %x_hbm.1, bf16[256,256]{1,0:T(8,128)(2,1)} %w_ref.1, bf16[1024,256]{1,0:T(8,128)(2,1)} %ct_hbm.1, bf16[5,8,128,128]{3,2,1,0:T(8,128)(2,1)} %bitcast.2, s32[2,1,5,8]{3,2,1,0:T(8,128)} %copy.9.coords_ref, ...), custom_call_target="tpu_custom_call" | custom-call | tf_op jit(solution)/shard_map/pallas_call | solution.py:491
  101.5 0.0 copy-start
  101.5 0.0 copy-start.1
  101.6 1.9 %copy.13 = bf16[1024,256]{1,0:T(8,128)(2,1)} copy(bf16[1024,256]{1,0:T(8,128)(2,1)} %get-tuple-element.12) | data formatting | bytes 1048576
  103.5 0.0 copy-done
  103.5 0.8 copy.14
  104.3 0.0 copy-done.1
  104.3 0.7 copy.15
Async XLA Ops:
  101.5 2.0 %copy-start = (bf16[1024,256]{1,0:T(8,128)(2,1)S(1)}, bf16[1024,256]{1,0:T(8,128)(2,1)}, u32[]{:S(2)}) copy-start(bf16[1024,256]{1,0:T(8,128)(2,1)} %get-tuple-element.13) | copy-start | bytes 1572868
  101.5 2.7 %copy-start.1 = (f32[2,8,16,256]{3,2,1,0:T(8,128)S(1)}, f32[2,8,16,256]{3,2,1,0:T(8,128)}, u32[]{:S(2)}) copy-start(f32[2,8,16,256]{3,2,1,0:T(8,128)} %get-tuple-element.8) | copy-start | bytes 786436

commit v3 on v2

--- a/solution.py
+++ b/solution.py
@@ -47,14 +47,11 @@
     v,
     xt,
     ws,
-    w0,
-    w1s,
     w1,
     w2,
     w3,
     wf,
     wp,
-    w1f,
     load_sem,
     out_sem,
     x_send,
@@ -97,9 +94,9 @@
     y_lo = me // (2 * ZS * XS)
     y = p * YL + y_lo
 
-    def z_peer(k):
+    def z_peer(k, core):
         other = lax.rem(z + k, ZS)
-        return other, (me + 2 * (other - z), p)
+        return core * ZS + other, (me + 2 * (other - z) + core - odd, p)
 
     def x_peer(k):
         other = lax.rem(x + k, XS)
@@ -109,10 +106,12 @@
         other = lax.rem(y + k, YL * reps)
         return other, (me + 2 * ZS * XS * (lax.rem(other, YL) - y_lo), other // YL)
 
-    z_peers = [z_peer(k) for k in range(1, ZS)]
+    z_peers = [z_peer(k, core) for k in range(1, ZS) for core in range(2)]
+    z_peers.append(((1 - odd) * ZS + z, (mate, p)))
+    spot = odd * ZS + z
     x_peers = [x_peer(k) for k in range(1, XS)]
     y_peers = [y_peer(k) for k in range(1, YL * reps)]
-    greet = [(up, p), (dn, p), (mate, p)] + [dev for _, dev in z_peers + x_peers + y_peers]
+    greet = [(up, p), (dn, p)] + [dev for _, dev in z_peers + x_peers + y_peers]
 
     barrier = pltpu.get_barrier_semaphore()
     for dev in greet:
@@ -407,59 +406,51 @@
     def w_wait(step, ref, slot):
         remote(ref, ref, w_send.at[step, 0], w_recv.at[step, slot], (mate, p)).wait_recv()
 
-    half, piece = f // 2, f // (2 * ZS)
-
     copies = rs_start(1, opp, a_last)
-    terms = matmul(xt[...], send[1]) * scale
-    wp[...] = terms
-    ws[...] = terms.astype(BF16)
-    w_go(0, 0, ws.at[rows((1 - odd) * half, half)], w0, 0, (mate, p))
+    piece = f // (2 * ZS)
+    wp[...] = (matmul(xt[...], send[1]) * scale).reshape(2 * ZS, piece, f)
+    ws[...] = wp[...].astype(BF16)
+    for other, dev in z_peers:
+        w_go(0, other, ws.at[other], w1.at[spot], spot, dev)
     last_hop = rs_middle(1, copies)
-    w_wait(0, w0, 0)
-    mine = wp[rows(odd * half, half), :] + w0[...].astype(F32)
-    w1f[...] = mine.reshape(ZS, piece, f)
-    w1s[...] = w1f[...].astype(BF16)
+    part = wp[spot]
     for other, dev in z_peers:
-        w_go(1, other, w1s.at[other], w1.at[z], z, dev)
-    part = w1f[z]
-    for other, dev in z_peers:
-        w_wait(1, w1.at[other], other)
+        w_wait(0, w1.at[other], other)
         part = part + w1[other].astype(F32)
     w2[x] = part.astype(BF16)
     for other, dev in x_peers:
-        w_go(2, other, w2.at[x], w2.at[x], x, dev)
+        w_go(1, other, w2.at[x], w2.at[x], x, dev)
+    for other, dev in x_peers:
+        w_wait(1, w2.at[other], other)
+    w3[y] = sum(w2[k].astype(F32) for k in range(XS)).astype(BF16)
+    for other, dev in y_peers:
+        w_go(2, other, w3.at[y], w3.at[y], y, dev)
     back = rs_finish(1, last_hop).astype(BF16)
     g[1, rows(p * q, q), :] = lax.dot_general(
         back, w, (((1,), (1,)), ((), ())), preferred_element_type=F32
     ).astype(BF16)
     ag_start(1)
     outs.append(store_out(len(outs), g.at[1], ig_hbm, p * q, q))
-    for other, dev in x_peers:
-        w_wait(2, w2.at[other], other)
-    w3[y] = sum(w2[k].astype(F32) for k in range(XS)).astype(BF16)
-    for other, dev in y_peers:
-        w_go(3, other, w3.at[y], w3.at[y], y, dev)
     ag_wait(1, 0)
     ag_wait(1, 1)
+    for other, dev in y_peers:
+        w_wait(2, w3.at[other], other)
+    wf[spot] = sum(w3[k].astype(F32) for k in range(YL * reps)).astype(BF16)
+    for other, dev in z_peers:
+        w_go(3, other, wf.at[spot], wf.at[spot], spot, dev)
     ag_wait(1, 2)
     outs.append(store_out(len(outs), g.at[1], ig_hbm, prv * q, q))
     ag_wait(1, 3)
     outs.append(store_out(len(outs), g.at[1], ig_hbm, nxt * q, q))
-    for other, dev in y_peers:
-        w_wait(3, w3.at[other], other)
-    wf[odd, z] = sum(w3[k].astype(F32) for k in range(YL * reps))
     for other, dev in z_peers:
-        w_go(4, other, wf.at[odd, z], wf.at[odd, z], z, dev)
+        w_wait(3, wf.at[other], other)
+    wp[...] = wf[...].astype(F32)
+    copy = pltpu.make_async_copy(wp, wg_hbm, out_sem.at[len(outs)])
+    copy.start()
+    outs.append(copy)
     ag_wait(1, 4)
     ag_wait(1, 5)
     outs.append(store_out(len(outs), g.at[1], ig_hbm, opp * q, q))
-    for other, dev in z_peers:
-        w_wait(4, wf.at[odd, other], other)
-    w_go(5, 0, wf.at[odd], wf.at[odd], 0, (mate, p))
-    w_wait(5, wf.at[1 - odd], 0)
-    copy = pltpu.make_async_copy(wf, wg_hbm, out_sem.at[len(outs)])
-    copy.start()
-    outs.append(copy)
 
     for copy in sent:
         copy.wait_send()
@@ -493,7 +484,7 @@
         out_shape=(
             jax.ShapeDtypeStruct((n, f), BF16),
             jax.ShapeDtypeStruct((n, f), BF16),
-            jax.ShapeDtypeStruct((2, ZS, piece, f), F32),
+            jax.ShapeDtypeStruct((2 * ZS, piece, f), F32),
         ),
         in_specs=[hbm, vmem, hbm, hbm, smem, smem],
         out_specs=(hbm, hbm, hbm),
@@ -514,15 +505,12 @@
             pltpu.VMEM((n, f), BF16),
             pltpu.VMEM((n, f), BF16),
             pltpu.VMEM((f, n), BF16),
-            pltpu.VMEM((f, f), BF16),
-            pltpu.VMEM((f // 2, f), BF16),
-            pltpu.VMEM((ZS, piece, f), BF16),
-            pltpu.VMEM((ZS, piece, f), BF16),
+            pltpu.VMEM((2 * ZS, piece, f), BF16),
+            pltpu.VMEM((2 * ZS, piece, f), BF16),
             pltpu.VMEM((XS, piece, f), BF16),
             pltpu.VMEM((YL * reps, piece, f), BF16),
-            pltpu.VMEM((2, ZS, piece, f), F32),
-            pltpu.VMEM((f, f), F32),
-            pltpu.VMEM((ZS, piece, f), F32),
+            pltpu.VMEM((2 * ZS, piece, f), BF16),
+            pltpu.VMEM((2 * ZS, piece, f), F32),
             dma((3,)),
             dma((16,)),
             dma((4, reps)),
@@ -533,8 +521,8 @@
             dma((2, 6)),
             dma((2, 6)),
             dma((2, 6)),
-            dma((6, 8)),
-            dma((6, 8)),
+            dma((4, 2 * ZS)),
+            dma((4, 2 * ZS)),
         ],
         compiler_params=pltpu.CompilerParams(
             collective_id=0, vmem_limit_bytes=56 << 20

time: 107 us -> 101 us (0.944); the launches traced: 105 us -> 100 us
  Pallas kernels: 99.6 us -> 94.8 us
    pallas_call x1, Pallas kernels: 99.6 us -> 94.8 us  [per_device(): pl.pallas_call(functools.partial(layer_kernel, groups, reps, (n * groups)...]
where the time goes in v3:
time: 101 us; the launch traced here: 100 us
  Pallas kernels  94.8 us (94%)
  local copies, waits for them, and re-layouts  4.74 us (5%)
    pallas_call x1, Pallas kernels, per_device(): pl.pallas_call(functools.partial(layer_kernel, groups, reps, (n * groups)...  94.8 us
    unnamed x8, local copies, waits for them, and re-layouts  4.74 us

profile of v3, /device:TPU:1, one launch (start us, length us, event | category | flops | bytes accessed | tf_op | source)
XLA Modules:
  0.0 100.2 jit_solution(11006581912833384628)
XLA Ops:
  0.6 1.3 %copy.9.coords_ref = s32[2,1,5,8]{3,2,1,0:T(8,128)} copy(s32[2,1,5,8]{3,1,2,0:T(1,128)} %param.10) | data formatting | bytes 640 | tf_op args[4]
  1.9 94.8 %shard_map.85 = (bf16[1024,256]{1,0:T(8,128)(2,1)}, bf16[1024,256]{1,0:T(8,128)(2,1)}, f32[16,16,256]{2,1,0:T(8,128)}) custom-call(bf16[1024,256]{1,0:T(8,128)(2,1)} %x_hbm.1, bf16[256,256]{1,0:T(8,128)(2,1)} %w_ref.1, bf16[1024,256]{1,0:T(8,128)(2,1)} %ct_hbm.1, bf16[5,8,128,128]{3,2,1,0:T(8,128)(2,1)} %bitcast.2, s32[2,1,5,8]{3,2,1,0:T(8,128)} %copy.9.coords_ref, ...), custom_call_target="tpu_custom_call" | custom-call | tf_op jit(solution)/shard_map/pallas_call | solution.py:482
  96.7 0.0 copy-start
  96.7 0.0 copy-start.1
  96.7 1.9 %copy.13 = bf16[1024,256]{1,0:T(8,128)(2,1)} copy(bf16[1024,256]{1,0:T(8,128)(2,1)} %get-tuple-element.12) | data formatting | bytes 1048576
  98.6 0.0 copy-done
  98.7 0.8 copy.14
  99.4 0.0 copy-done.1
  99.4 0.7 copy.15
Async XLA Ops:
  96.7 2.0 %copy-start = (bf16[1024,256]{1,0:T(8,128)(2,1)S(1)}, bf16[1024,256]{1,0:T(8,128)(2,1)}, u32[]{:S(2)}) copy-start(bf16[1024,256]{1,0:T(8,128)(2,1)} %get-tuple-element.13) | copy-start | bytes 1572868
  96.7 2.7 %copy-start.1 = (f32[16,16,256]{2,1,0:T(8,128)S(1)}, f32[16,16,256]{2,1,0:T(8,128)}, u32[]{:S(2)}) copy-start(f32[16,16,256]{2,1,0:T(8,128)} %get-tuple-element.8) | copy-start | bytes 786436

commit v4 on v3

--- a/solution.py
+++ b/solution.py
@@ -27,9 +27,9 @@
     tiles_hbm,
     coords_ref,
     counts_ref,
-    act_hbm,
-    ig_hbm,
-    wg_hbm,
+    act_ref,
+    ig_ref,
+    wg_ref,
     px,
     ad,
     dense,
@@ -43,7 +43,6 @@
     rf,
     g,
     ctv,
-    actv,
     v,
     xt,
     ws,
@@ -53,7 +52,6 @@
     wf,
     wp,
     load_sem,
-    out_sem,
     x_send,
     x_recv,
     a_send,
@@ -138,10 +136,11 @@
         remote(part, part, ssem.at[0, chunk], rsem.at[slot, chunk], (mate, p)).wait_recv()
 
     def x_copy(kind, chunk):
-        return panel_copy(x_hbm, px, x_send, x_recv, kind, chunk, q)
-
-    def x_wait(slot, chunk):
-        panel_wait(px, x_send, x_recv, slot, chunk, q)
+        return panel_copy(x_hbm, px, x_send, x_recv, kind, chunk, h)
+
+    def x_wait(slot, at):
+        panel_wait(px, x_send, x_recv, slot, 2 * at, h)
+        panel_wait(px, x_send, x_recv, slot, 2 * at + 1, h)
 
     def a_copy(kind, chunk):
         return panel_copy(ad.at[2], ad, a_send, a_recv, kind, chunk, h)
@@ -150,15 +149,16 @@
         panel_wait(ad, a_send, a_recv, slot, 2 * at, h)
         panel_wait(ad, a_send, a_recv, slot, 2 * at + 1, h)
 
-    def x_forward(chunk):
-        x_wait(fwd_slot, chunk)
-        x_copy(3, chunk).start()
+    def x_forward(at):
+        for half in range(2):
+            panel_wait(px, x_send, x_recv, fwd_slot, 2 * at + half, h)
+            x_copy(3, 2 * at + half).start()
 
     def a_forward(chunk):
         panel_wait(ad, a_send, a_recv, fwd_slot, chunk, h)
         a_copy(3, chunk).start()
 
-    @pl.loop(0, reps)
+    @pl.loop(0, 2 * reps)
     def _(i):
         for kind in range(3):
             x_copy(kind, i).start()
@@ -222,15 +222,13 @@
             total = term if total is None else total + term
         acc[...] = total
 
-    def rs_start(ph, chunk, panels):
+    def rs_start(ph, chunk, panel):
         ssem, rsem = rs_send.at[ph], rs_recv.at[ph]
         buf = send.at[ph]
 
         def block(at):
             part = rows(at * q, q)
-            total = acc[part, :]
-            for slot, panel in panels:
-                total = total + matmul(dense[slot, chunk, part, :], panel())
+            total = acc[part, :] + matmul(dense[out_slot, chunk, part, :], panel())
             acc[part, :] = total
             buf[part, :] = total.astype(BF16)
 
@@ -273,16 +271,15 @@
         absorb(out_slot, i, x_panel(out_slot, i))
 
     last = reps - 1
-    v[pl.ds(0, q), :] = x_panel(fwd_slot, last)
     x_wait(far_slot, last)
-    v[pl.ds(q, q), :] = x_panel(far_slot, last)
+
+    @pl.loop(0, 2)
+    def _(i):
+        slot = jnp.where(i == 0, fwd_slot, far_slot)
+        absorb(slot, last, x_panel(slot, last))
+
     x_wait(out_slot, last)
-    v[pl.ds(2 * q, q), :] = x_panel(out_slot, last)
-    x_last = [
-        (fwd_slot, lambda: v[pl.ds(0, q), :]),
-        (far_slot, lambda: v[pl.ds(q, q), :]),
-        (out_slot, lambda: v[pl.ds(2 * q, q), :]),
-    ]
+    v[pl.ds(0, q), :] = x_panel(out_slot, last)
 
     def rs_middle(ph, copies):
         ssem, rsem = rs_send.at[ph], rs_recv.at[ph]
@@ -316,15 +313,11 @@
         if k < 2:
             go(ag_copy(ph, 4 + k, at, half, (nxt, prv)[k]))
 
-    def store_out(k, src, dst, start, size):
+    def store_out(start, size):
         part = rows(start, size)
-        copy = pltpu.make_async_copy(src.at[part], dst.at[part], out_sem.at[k])
-        copy.start()
-        return copy
-
-    outs = []
-
-    g[0, rows(p * q, q), :] = rs_finish(0, rs_middle(0, rs_start(0, last, x_last))).astype(BF16)
+        ig_ref[part, :] = g[1, part, :]
+
+    g[0, rows(p * q, q), :] = rs_finish(0, rs_middle(0, rs_start(0, last, lambda: v[pl.ds(0, q), :]))).astype(BF16)
     ag_start(0)
     loads[2].wait()
 
@@ -336,8 +329,7 @@
         ad[2, part, :] = (ctv[part, :].astype(F32) * (sig * (1.0 + value * (1.0 - sig)))).astype(BF16)
         for kind in range(3):
             a_copy(kind, 2 * at + half).start()
-        actv[part, :] = (value * sig).astype(BF16)
-        outs.append(store_out(len(outs), actv, act_hbm, start, h))
+        act_ref[part, :] = (value * sig).astype(BF16)
 
     def a_panel(slot, chunk):
         return ad[slot, rows(chunk * q, q), :]
@@ -397,8 +389,13 @@
     a_forward(2 * opp)
     a_forward(2 * opp + 1)
     a_wait(far_slot, opp)
+
+    @pl.loop(0, 2)
+    def _(i):
+        slot = jnp.where(i == 0, fwd_slot, far_slot)
+        absorb(slot, opp, a_panel(slot, opp))
+
     a_wait(out_slot, opp)
-    a_last = [(slot, functools.partial(a_panel, slot, opp)) for slot in (fwd_slot, far_slot, out_slot)]
 
     def w_go(step, to, src, dst, slot, dev):
         go(remote(src, dst, w_send.at[step, to], w_recv.at[step, slot], dev))
@@ -406,7 +403,7 @@
     def w_wait(step, ref, slot):
         remote(ref, ref, w_send.at[step, 0], w_recv.at[step, slot], (mate, p)).wait_recv()
 
-    copies = rs_start(1, opp, a_last)
+    copies = rs_start(1, opp, lambda: a_panel(out_slot, opp))
     piece = f // (2 * ZS)
     wp[...] = (matmul(xt[...], send[1]) * scale).reshape(2 * ZS, piece, f)
     ws[...] = wp[...].astype(BF16)
@@ -430,7 +427,7 @@
         back, w, (((1,), (1,)), ((), ())), preferred_element_type=F32
     ).astype(BF16)
     ag_start(1)
-    outs.append(store_out(len(outs), g.at[1], ig_hbm, p * q, q))
+    store_out(p * q, q)
     ag_wait(1, 0)
     ag_wait(1, 1)
     for other, dev in y_peers:
@@ -439,34 +436,24 @@
     for other, dev in z_peers:
         w_go(3, other, wf.at[spot], wf.at[spot], spot, dev)
     ag_wait(1, 2)
-    outs.append(store_out(len(outs), g.at[1], ig_hbm, prv * q, q))
+    store_out(prv * q, q)
     ag_wait(1, 3)
-    outs.append(store_out(len(outs), g.at[1], ig_hbm, nxt * q, q))
+    store_out(nxt * q, q)
     for other, dev in z_peers:
         w_wait(3, wf.at[other], other)
-    wp[...] = wf[...].astype(F32)
-    copy = pltpu.make_async_copy(wp, wg_hbm, out_sem.at[len(outs)])
-    copy.start()
-    outs.append(copy)
+    wg_ref[...] = wf[...].astype(F32)
     ag_wait(1, 4)
     ag_wait(1, 5)
-    outs.append(store_out(len(outs), g.at[1], ig_hbm, opp * q, q))
+    store_out(opp * q, q)
 
     for copy in sent:
         copy.wait_send()
 
-    @pl.loop(0, reps)
+    @pl.loop(0, 2 * reps)
     def _(i):
         for kind in range(4):
             x_copy(kind, i).wait_send()
-
-    @pl.loop(0, 2 * reps)
-    def _(i):
-        for kind in range(4):
             a_copy(kind, i).wait_send()
-
-    for copy in outs:
-        copy.wait()
 
 
 def per_device(groups, reps, node_feats, weight, cotangent, tile_values, tile_coords, tile_counts):
@@ -482,12 +469,12 @@
     activated, input_grad, weight_grad = pl.pallas_call(
         functools.partial(layer_kernel, groups, reps, (n * groups) ** (-0.5)),
         out_shape=(
-            jax.ShapeDtypeStruct((n, f), BF16),
-            jax.ShapeDtypeStruct((n, f), BF16),
-            jax.ShapeDtypeStruct((2 * ZS, piece, f), F32),
+            pltpu.VMEM((n, f), BF16),
+            pltpu.VMEM((n, f), BF16),
+            pltpu.VMEM((2 * ZS, piece, f), F32),
         ),
         in_specs=[hbm, vmem, hbm, hbm, smem, smem],
-        out_specs=(hbm, hbm, hbm),
+        out_specs=(vmem, vmem, vmem),
         scratch_shapes=[
             pltpu.VMEM((reach, n, f), BF16),
             pltpu.VMEM((reach, n, f), BF16),
@@ -503,7 +490,6 @@
             pltpu.VMEM((2, n, f), BF16),
             pltpu.VMEM((n, f), BF16),
             pltpu.VMEM((n, f), BF16),
-            pltpu.VMEM((n, f), BF16),
             pltpu.VMEM((f, n), BF16),
             pltpu.VMEM((2 * ZS, piece, f), BF16),
             pltpu.VMEM((2 * ZS, piece, f), BF16),
@@ -512,9 +498,8 @@
             pltpu.VMEM((2 * ZS, piece, f), BF16),
             pltpu.VMEM((2 * ZS, piece, f), F32),
             dma((3,)),
-            dma((16,)),
-            dma((4, reps)),
-            dma((reach, reps)),
+            dma((4, 2 * reps)),
+            dma((reach, 2 * reps)),
             dma((4, 2 * reps)),
             dma((reach, 2 * reps)),
             dma((2, 6)),

time: 101 us -> 99 us (0.980)
  local copies, waits for them, and re-layouts: 4.74 us -> 3.58 us
    unnamed x8 -> x4, local copies, waits for them, and re-layouts: 4.74 us -> 3.58 us
where the time goes in v4:
time: 99 us; the launch traced here: 98.8 us
  Pallas kernels  94.6 us (96%)
  local copies, waits for them, and re-layouts  3.58 us (4%)
    pallas_call x1, Pallas kernels, per_device(): pl.pallas_call(functools.partial(layer_kernel, groups, reps, (n * groups)...  94.6 us
    unnamed x4, local copies, waits for them, and re-layouts  3.58 us

profile of v4, /device:TPU:1, one launch (start us, length us, event | category | flops | bytes accessed | tf_op | source)
XLA Modules:
  0.0 98.8 jit_solution(8022429861950919155)
XLA Ops:
  0.6 1.3 %copy.9.coords_ref = s32[2,1,5,8]{3,2,1,0:T(8,128)} copy(s32[2,1,5,8]{3,1,2,0:T(1,128)} %param.10) | data formatting | bytes 640 | tf_op args[4]
  1.9 94.6 %shard_map.85 = (bf16[1024,256]{1,0:T(8,128)(2,1)S(1)}, bf16[1024,256]{1,0:T(8,128)(2,1)S(1)}, f32[16,16,256]{2,1,0:T(8,128)S(1)}) custom-call(bf16[1024,256]{1,0:T(8,128)(2,1)} %x_hbm.1, bf16[256,256]{1,0:T(8,128)(2,1)} %w_ref.1, bf16[1024,256]{1,0:T(8,128)(2,1)} %ct_hbm.1, bf16[5,8,128,128]{3,2,1,0:T(8,128)(2,1)} %bitcast.3, ...), custom_call_target="tpu_custom_call" | custom-call | tf_op jit(solution)/shard_map/pallas_call | solution.py:469
  96.5 0.8 copy.13
  97.3 0.7 copy.15
  98.0 0.8 copy.14
